TPU v7x, 128 devices: a whole 4x4x4 slice. The times are simulated.
128 devices in a mesh: layer: 4 (over x), node: 32 (over y, z, core).
Axes of the slice: x: 4, y: 4, z: 4, core: 2. Of those that a mesh axis runs over, the one named last changes fastest.
Arguments:
- features: bfloat16 [4, 8192, 512], P(None, 'node'), may hold values from -6 to 6
- w_self: bfloat16 [4, 512, 512], P('layer'), may hold values from -0.1875 to 0.1875
- w_neigh: bfloat16 [4, 512, 512], P('layer'), may hold values from -0.1875 to 0.1875
- w_out: bfloat16 [512, 172], replicated, may hold values from -0.25 to 0.25
- labels: int32 [4, 8192], P(None, 'node'), may hold values from 0 to 171
- train_mask: int32 [4, 8192], P(None, 'node'), may hold values 0 or 1
- tile_cols: int32 [4, 32, 2, 4], P(None, 'node'), may hold values from 0 to 3
- tile_vals: bfloat16 [4, 32, 2, 4, 128, 128], P(None, 'node'), may hold values from -0.25 to 0.25
- send_rows: int32 [4, 32, 32, 8], P(None, 'node'), may hold values from 0 to 255
- send_counts: int32 [4, 32, 32], P(None, 'node'), may hold values from 0 to 8, as said below
Outputs:
- layer_acts: bfloat16 [4, 4, 8192, 512], P('layer', None, 'node')
- act_grads: bfloat16 [4, 4, 8192, 512], P('layer', None, 'node')
- grad_self: float32 [4, 512, 512], P('layer')
- grad_neigh: float32 [4, 512, 512], P('layer')
Inputs may be any that keep to these rules, and one draw needn't show every extreme that they name: `send_counts`: in every span one partition, drawn per span, gets 8 rows from every partition, itself included; the other counts are at most 4. `send_rows`: entries of slots at or past the count are ignored; rows may repeat. `tile_cols`: A value below 2 is a tile of the partition's own rows; larger values are tiles of the received rows in source order, 8 slots per source, then zero rows; tiles of a row tile may repeat.
All inputs are finite; a program needn't handle non-finite values. No bound on the sum of `train_mask` on one device may be relied on, other than what follows from the above.
Results may differ from a plain program's by a relative error of at most 0.03.
Values may be sent and summed in bfloat16 or wider, within the bound.
No kernel may reach another device: no remote copies, remote signals or barrier semaphores. Data moves between devices by JAX's collectives and lax.ppermute only.
A program may use at most 128 MiB of HBM per device.

v0:
```python
import jax
import jax.numpy as jnp
from jax import lax
from jax.sharding import PartitionSpec as P


def from_behind(value, axis, steps):
    count = lax.axis_size(axis)
    first, last = (max(0, -steps), min(count, count - steps))
    return lax.ppermute(value, axis, [(source, source + steps) for source in range(first, last)])


def silu_slope(preact):
    sigma = jax.nn.sigmoid(preact)
    return sigma * (1.0 + preact * (1.0 - sigma))


def pick(array, index):
    return lax.dynamic_index_in_dim(array, index, 0, keepdims=False)


def put_row(buffer, value, index, valid):
    current = pick(buffer, index)
    return lax.dynamic_update_index_in_dim(buffer, jnp.where(valid, value, current), index, 0)


def live_slots(send_list, counts):
    return jnp.arange(send_list.shape[1])[None, :] < counts[:, None]


def layer_forward(hidden_in, weight_self, weight_neigh, col_tiles, values, send_list, counts):
    feat_dim = hidden_in.shape[1]
    tile_size = values.shape[-1]
    is_live = live_slots(send_list, counts)
    outgoing = jnp.where(
        is_live[:, :, None], jnp.take(hidden_in, send_list, axis=0), jnp.zeros((), hidden_in.dtype)
    )
    arrived = lax.all_to_all(outgoing, "node", split_axis=0, concat_axis=0, tiled=True)
    extended = jnp.concatenate([hidden_in, arrived.reshape(-1, feat_dim)], axis=0)
    blocks = jnp.take(extended.reshape(-1, tile_size, feat_dim), col_tiles, axis=0)
    summed = jnp.einsum("rkij,rkjd->rid", values, blocks, preferred_element_type=jnp.float32)
    aggregate = summed.reshape(hidden_in.shape).astype(jnp.bfloat16)
    preact = jnp.dot(hidden_in, weight_self, preferred_element_type=jnp.float32)
    preact = preact + jnp.dot(aggregate, weight_neigh, preferred_element_type=jnp.float32)
    return (aggregate, preact, jax.nn.silu(preact).astype(jnp.bfloat16))


def layer_backward(
    d_out,
    hidden_in,
    aggregate,
    preact,
    weight_self,
    weight_neigh,
    col_tiles,
    values,
    send_list,
    counts,
):
    node_rows, feat_dim = hidden_in.shape
    row_tiles, degree, tile_size = (values.shape[0], values.shape[1], values.shape[-1])
    peers, slot_count = send_list.shape
    d_pre = (d_out.astype(jnp.float32) * silu_slope(preact)).astype(jnp.bfloat16)
    over_rows = (((0,), (0,)), ((), ()))
    over_cols = (((1,), (1,)), ((), ()))
    g_self = lax.dot_general(hidden_in, d_pre, over_rows, preferred_element_type=jnp.float32)
    g_neigh = lax.dot_general(aggregate, d_pre, over_rows, preferred_element_type=jnp.float32)
    back_self = lax.dot_general(d_pre, weight_self, over_cols, preferred_element_type=jnp.float32)
    d_agg = lax.dot_general(
        d_pre, weight_neigh, over_cols, preferred_element_type=jnp.float32
    ).astype(jnp.bfloat16)
    pieces = jnp.einsum(
        "rkij,rid->rkjd",
        values,
        d_agg.reshape(row_tiles, tile_size, feat_dim),
        preferred_element_type=jnp.float32,
    )
    col_count = (node_rows + peers * slot_count + tile_size - 1) // tile_size
    selector = (col_tiles.reshape(-1)[None, :] == jnp.arange(col_count)[:, None]).astype(
        jnp.float32
    )
    d_ext = jnp.einsum(
        "cn,njd->cjd",
        selector,
        pieces.reshape(row_tiles * degree, tile_size, feat_dim),
        precision=lax.Precision.HIGHEST,
    )
    d_ext = d_ext.reshape(-1, feat_dim)
    local_part = d_ext[:node_rows]
    remote = (
        d_ext[node_rows : node_rows + peers * slot_count]
        .reshape(peers, slot_count, feat_dim)
        .astype(jnp.bfloat16)
    )
    returned = lax.all_to_all(remote, "node", split_axis=0, concat_axis=0, tiled=True)
    is_live = live_slots(send_list, counts)
    masked = jnp.where(
        is_live[:, :, None], returned.astype(jnp.float32), jnp.zeros((), jnp.float32)
    )
    scattered = jax.ops.segment_sum(
        masked.reshape(-1, feat_dim), send_list.reshape(-1), num_segments=node_rows
    )
    d_in = (back_self + local_part + scattered).astype(jnp.bfloat16)
    return (d_in, g_self, g_neigh)


def finish_grads(grad_pair, scale):
    summed = (
        lax.psum(grad_pair[0].astype(jnp.bfloat16), "node").astype(jnp.float32),
        lax.psum(grad_pair[1].astype(jnp.bfloat16), "node").astype(jnp.float32),
    )
    return (summed[0] * scale, summed[1] * scale)


def body(
    features,
    w_self,
    w_neigh,
    w_out,
    labels,
    train_mask,
    tile_cols,
    tile_vals,
    send_rows,
    send_counts,
):
    my_section = lax.axis_index("layer")
    sections = lax.axis_size("layer")
    spans, node_rows, feat_dim = features.shape
    classes = w_out.shape[1]
    scale = 1.0 / (spans * node_rows * lax.axis_size("node"))

    def graph_of(span_idx):
        return (
            pick(tile_cols, span_idx)[0],
            pick(tile_vals, span_idx)[0],
            pick(send_rows, span_idx)[0],
            pick(send_counts, span_idx)[0],
        )

    rows_zero = jnp.zeros((node_rows, feat_dim), jnp.bfloat16)
    block_bf = jnp.zeros((spans, node_rows, feat_dim), jnp.bfloat16)
    block_f32 = jnp.zeros((spans, node_rows, feat_dim), jnp.float32)
    square_zero = jnp.zeros((feat_dim, feat_dim), jnp.float32)
    weight_self = w_self[0]
    weight_neigh = w_neigh[0]
    steps_total = spans + sections - 1

    def forward_step(step, carry):
        incoming, saved_in, saved_agg, saved_pre, acts = carry
        span_idx = step - my_section
        valid = (span_idx >= 0) & (span_idx < spans)
        safe_idx = jnp.clip(span_idx, 0, spans - 1)
        hidden_in = jnp.where(my_section == 0, pick(features, safe_idx), incoming)
        aggregate, preact, hidden_out = layer_forward(
            hidden_in, weight_self, weight_neigh, *graph_of(safe_idx)
        )
        saved_in = put_row(saved_in, hidden_in, safe_idx, valid)
        saved_agg = put_row(saved_agg, aggregate, safe_idx, valid)
        saved_pre = put_row(saved_pre, preact, safe_idx, valid)
        acts = put_row(acts, hidden_out, safe_idx, valid)
        outgoing = from_behind(hidden_out, "layer", 1)
        return (outgoing, saved_in, saved_agg, saved_pre, acts)

    start = (rows_zero, block_bf, block_bf, block_f32, block_bf)
    fwd_done = lax.fori_loop(0, steps_total, forward_step, start)
    saved_in, saved_agg, saved_pre, acts = (fwd_done[1], fwd_done[2], fwd_done[3], fwd_done[4])
    logits = jnp.einsum("...d,dc->...c", acts, w_out, preferred_element_type=jnp.float32)
    expo = jnp.exp(logits)
    probs = expo / jnp.sum(expo, axis=-1, keepdims=True)
    onehot = (labels[..., None] == jnp.arange(classes)).astype(jnp.float32)
    g_logits = (train_mask[..., None].astype(jnp.float32) * (probs - onehot)).astype(jnp.bfloat16)
    d_top = jnp.einsum("...c,dc->...d", g_logits, w_out, preferred_element_type=jnp.float32).astype(
        jnp.bfloat16
    )

    def backward_step(step, carry):
        incoming, sum_self, sum_neigh, grads_out = carry
        span_idx = step - (sections - 1 - my_section)
        valid = (span_idx >= 0) & (span_idx < spans)
        safe_idx = jnp.clip(span_idx, 0, spans - 1)
        d_out = jnp.where(my_section == sections - 1, pick(d_top, safe_idx), incoming)
        hidden_in = pick(saved_in, safe_idx)
        graph = graph_of(safe_idx)
        aggregate = pick(saved_agg, safe_idx)
        preact = pick(saved_pre, safe_idx)
        d_in, g_self, g_neigh = layer_backward(
            d_out, hidden_in, aggregate, preact, weight_self, weight_neigh, *graph
        )
        sum_self = sum_self + jnp.where(valid, g_self, 0.0)
        sum_neigh = sum_neigh + jnp.where(valid, g_neigh, 0.0)
        grads_out = put_row(grads_out, d_in, safe_idx, valid)
        outgoing = from_behind(d_in, "layer", -1)
        return (outgoing, sum_self, sum_neigh, grads_out)

    bwd_done = lax.fori_loop(
        0, steps_total, backward_step, (rows_zero, square_zero, square_zero, block_bf)
    )
    grad_self, grad_neigh = finish_grads((bwd_done[1][None], bwd_done[2][None]), scale)
    return (acts[None], bwd_done[3][None], grad_self, grad_neigh)


def solution(mesh):
    in_specs = (
        P(None, "node", None),
        P("layer", None, None),
        P("layer", None, None),
        P(),
        P(None, "node"),
        P(None, "node"),
        P(None, "node", None, None),
        P(None, "node", None, None, None, None),
        P(None, "node", None, None),
        P(None, "node", None),
    )
    out_specs = (
        P("layer", None, "node", None),
        P("layer", None, "node", None),
        P("layer", None, None),
        P("layer", None, None),
    )
    return jax.shard_map(body, mesh=mesh, in_specs=in_specs, out_specs=out_specs, check_vma=False)
```

profile of v0, /device:TPU:1, one launch (start us, length us, event | category | flops | bytes accessed | tf_op | source)
XLA Modules:
  0.0 613.9 jit_solution(9725740799689017812)
XLA Ops:
  12.6 233.1 %while.44 = (s32[]{:T(128)}, bf16[256,512]{1,0:T(8,128)(2,1)S(1)}, bf16[4,256,512]{2,1,0:T(8,128)(2,1)}, bf16[4,256,512]{2,1,0:T(8,128)(2,1)}, f32[4,256,512]{2,...) while((s32[]{:T(128)}, bf16[256,512]{1,0:T(8,128)(2,1)S(1)}, ...), condition=%wide.region_1.2_spmd, body=%wide.region_0.1_spmd.sunk | while | flops 406065728 | bytes 27805224 | solution.py:166
  17.8 9.6 %all-to-all-start = ((bf16[32,8,512]{2,1,0:T(8,128)(2,1)}), bf16[32,8,512]{2,1,0:T(8,128)(2,1)S(1)}, u32[]{:S(2)}, u32[]{:S(2)}) async-start(bf16[32,8,512]{2,1,0:T(8,128)(2,1)} %fusion.105), calls=%async_computation | async-start | bytes 524288 | tf_op jit(solution)/shard_map/while/body/eval_jaxpr/all_to_all | solution.py:38
  29.8 6.6 %all-to-all-done = bf16[32,8,512]{2,1,0:T(8,128)(2,1)S(1)} async-done(((bf16[32,8,512]{2,1,0:T(8,128)(2,1)}), bf16[32,8,512]{2,1,0:T(8,128)(2,1)S(1)}, u32[]{:S(2)}, u32[]{:S(2)}) %all-to-all-start) | async-done | bytes 262176 | tf_op jit(solution)/shard_map/while/body/eval_jaxpr/all_to_all | solution.py:38
  61.4 6.8 %all-to-all-done = bf16[32,8,512]{2,1,0:T(8,128)(2,1)S(1)} async-done(((bf16[32,8,512]{2,1,0:T(8,128)(2,1)}), bf16[32,8,512]{2,1,0:T(8,128)(2,1)S(1)}, u32[]{:S(2)}, u32[]{:S(2)}) %all-to-all-start) | async-done | bytes 262176 | tf_op jit(solution)/shard_map/while/body/eval_jaxpr/all_to_all | solution.py:38
  94.1 6.8 %all-to-all-done = bf16[32,8,512]{2,1,0:T(8,128)(2,1)S(1)} async-done(((bf16[32,8,512]{2,1,0:T(8,128)(2,1)}), bf16[32,8,512]{2,1,0:T(8,128)(2,1)S(1)}, u32[]{:S(2)}, u32[]{:S(2)}) %all-to-all-start) | async-done | bytes 262176 | tf_op jit(solution)/shard_map/while/body/eval_jaxpr/all_to_all | solution.py:38
  126.8 6.8 %all-to-all-done = bf16[32,8,512]{2,1,0:T(8,128)(2,1)S(1)} async-done(((bf16[32,8,512]{2,1,0:T(8,128)(2,1)}), bf16[32,8,512]{2,1,0:T(8,128)(2,1)S(1)}, u32[]{:S(2)}, u32[]{:S(2)}) %all-to-all-start) | async-done | bytes 262176 | tf_op jit(solution)/shard_map/while/body/eval_jaxpr/all_to_all | solution.py:38
  159.5 6.8 %all-to-all-done = bf16[32,8,512]{2,1,0:T(8,128)(2,1)S(1)} async-done(((bf16[32,8,512]{2,1,0:T(8,128)(2,1)}), bf16[32,8,512]{2,1,0:T(8,128)(2,1)S(1)}, u32[]{:S(2)}, u32[]{:S(2)}) %all-to-all-start) | async-done | bytes 262176 | tf_op jit(solution)/shard_map/while/body/eval_jaxpr/all_to_all | solution.py:38
  192.2 6.8 %all-to-all-done = bf16[32,8,512]{2,1,0:T(8,128)(2,1)S(1)} async-done(((bf16[32,8,512]{2,1,0:T(8,128)(2,1)}), bf16[32,8,512]{2,1,0:T(8,128)(2,1)S(1)}, u32[]{:S(2)}, u32[]{:S(2)}) %all-to-all-start) | async-done | bytes 262176 | tf_op jit(solution)/shard_map/while/body/eval_jaxpr/all_to_all | solution.py:38
  224.9 6.8 %all-to-all-done = bf16[32,8,512]{2,1,0:T(8,128)(2,1)S(1)} async-done(((bf16[32,8,512]{2,1,0:T(8,128)(2,1)}), bf16[32,8,512]{2,1,0:T(8,128)(2,1)S(1)}, u32[]{:S(2)}, u32[]{:S(2)}) %all-to-all-start) | async-done | bytes 262176 | tf_op jit(solution)/shard_map/while/body/eval_jaxpr/all_to_all | solution.py:38
  249.5 247.1 %while.45 = (s32[]{:T(128)}, bf16[256,512]{1,0:T(8,128)(2,1)}, f32[512,512]{1,0:T(8,128)}, f32[512,512]{1,0:T(8,128)}, bf16[4,256,512]{2,1,0:T(8,128)(2,1)}, /*i...) while((s32[]{:T(128)}, bf16[256,512]{1,0:T(8,128)(2,1)}, ...), condition=%wide.region_5.6_spmd.clone, body=%wide.region_3.5_spmd.clone.sunk | while | flops 700186880 | bytes 31204564 | solution.py:196
  257.0 5.2 all-to-all-start.1
  266.3 5.0 all-to-all-done.1
  277.6 8.1 %collective-permute-done.1 = bf16[256,512]{1,0:T(8,128)(2,1)} collective-permute-done((bf16[256,512]{1,0:T(8,128)(2,1)S(1)}, bf16[256,512]{1,0:T(8,128)(2,1)}, u32[]{:S(2)}, u32[]{:S(2)}) %collective-permute-start.1) | collective-permute-done | bytes 262176 | tf_op jit(solution)/shard_map/while/body/eval_jaxpr/ppermute | solution.py:10
  293.3 4.8 all-to-all-start.1
  302.6 4.7 all-to-all-done.1
  313.6 7.1 %collective-permute-done.1 = bf16[256,512]{1,0:T(8,128)(2,1)} collective-permute-done((bf16[256,512]{1,0:T(8,128)(2,1)S(1)}, bf16[256,512]{1,0:T(8,128)(2,1)}, u32[]{:S(2)}, u32[]{:S(2)}) %collective-permute-start.1) | collective-permute-done | bytes 262176 | tf_op jit(solution)/shard_map/while/body/eval_jaxpr/ppermute | solution.py:10
  328.2 5.2 all-to-all-start.1
  337.8 4.7 all-to-all-done.1
  348.8 7.1 %collective-permute-done.1 = bf16[256,512]{1,0:T(8,128)(2,1)} collective-permute-done((bf16[256,512]{1,0:T(8,128)(2,1)S(1)}, bf16[256,512]{1,0:T(8,128)(2,1)}, u32[]{:S(2)}, u32[]{:S(2)}) %collective-permute-start.1) | collective-permute-done | bytes 262176 | tf_op jit(solution)/shard_map/while/body/eval_jaxpr/ppermute | solution.py:10
  363.4 5.2 all-to-all-start.1
  373.0 4.7 all-to-all-done.1
  383.9 7.1 %collective-permute-done.1 = bf16[256,512]{1,0:T(8,128)(2,1)} collective-permute-done((bf16[256,512]{1,0:T(8,128)(2,1)S(1)}, bf16[256,512]{1,0:T(8,128)(2,1)}, u32[]{:S(2)}, u32[]{:S(2)}) %collective-permute-start.1) | collective-permute-done | bytes 262176 | tf_op jit(solution)/shard_map/while/body/eval_jaxpr/ppermute | solution.py:10
  398.5 5.2 all-to-all-start.1
  408.2 4.7 all-to-all-done.1
  419.1 7.1 %collective-permute-done.1 = bf16[256,512]{1,0:T(8,128)(2,1)} collective-permute-done((bf16[256,512]{1,0:T(8,128)(2,1)S(1)}, bf16[256,512]{1,0:T(8,128)(2,1)}, u32[]{:S(2)}, u32[]{:S(2)}) %collective-permute-start.1) | collective-permute-done | bytes 262176 | tf_op jit(solution)/shard_map/while/body/eval_jaxpr/ppermute | solution.py:10
  433.7 5.2 all-to-all-start.1
  443.4 4.7 all-to-all-done.1
  454.3 7.1 %collective-permute-done.1 = bf16[256,512]{1,0:T(8,128)(2,1)} collective-permute-done((bf16[256,512]{1,0:T(8,128)(2,1)S(1)}, bf16[256,512]{1,0:T(8,128)(2,1)}, u32[]{:S(2)}, u32[]{:S(2)}) %collective-permute-start.1) | collective-permute-done | bytes 262176 | tf_op jit(solution)/shard_map/while/body/eval_jaxpr/ppermute | solution.py:10
  468.9 5.2 all-to-all-start.1
  478.6 4.7 all-to-all-done.1
  489.5 7.1 %collective-permute-done.1 = bf16[256,512]{1,0:T(8,128)(2,1)} collective-permute-done((bf16[256,512]{1,0:T(8,128)(2,1)S(1)}, bf16[256,512]{1,0:T(8,128)(2,1)}, u32[]{:S(2)}, u32[]{:S(2)}) %collective-permute-start.1) | collective-permute-done | bytes 262176 | tf_op jit(solution)/shard_map/while/body/eval_jaxpr/ppermute | solution.py:10
  499.2 103.5 %all-reduce.3.cloned.1.call-done = (bf16[1,512,512]{2,1,0:T(8,128)(2,1)}, bf16[1,512,512]{2,1,0:T(8,128)(2,1)}) async-done(((bf16[1,512,512]{2,1,0:T(8,128)(2,1)}, bf16[1,512,512]{2,1,0:T(8,128)(2,1)}), (bf16[1,512,512]{2,1,0:T(8,128)(2,1)}, bf16[1,512,512]{2,1,0:T(8,128)(2,1)})) %all-reduce.3.cloned.1.call-update) | async-done | bytes 1048592 | tf_op jit(solution)/shard_map/psum | solution.py:109
  (421 shorter events, 318.2 us)
Async XLA Ops:
  7.2 238.5 %copy-start = (bf16[512,172]{0,1:T(8,128)(2,1)S(1)}, bf16[512,172]{0,1:T(8,128)(2,1)}, u32[]{:S(2)}) copy-start(bf16[512,172]{0,1:T(8,128)(2,1)} %param.17) | copy-start | bytes 528388
  7.2 595.6 %all-reduce.3.cloned.1.call-start = ((), (), s32[]{:S(2)}) async-start(), calls=%async_computation.2 | async-start | bytes 2097152 | tf_op jit(solution)/shard_map/psum | solution.py:109
  12.6 233.6 %copy-start.9 = (s32[4,256]{1,0:T(4,128)S(1)}, s32[4,256]{1,0:T(4,128)}, u32[]{:S(2)}) copy-start(s32[4,256]{1,0:T(4,128)} %param.18) | copy-start | bytes 12292
  12.6 14.9 %copy-start.5 = (bf16[4,256,512]{2,1,0:T(8,128)(2,1)}, bf16[4,256,512]{2,1,0:T(8,128)(2,1)S(1)}, u32[]{:S(2)}) copy-start(bf16[4,256,512]{2,1,0:T(8,128)(2,1)S(1)} %get-tuple-element.1101) | copy-start | bytes 3145732 | tf_op jit(solution)/shard_map/while
  17.8 18.6 %all-to-all-start = ((bf16[32,8,512]{2,1,0:T(8,128)(2,1)}), bf16[32,8,512]{2,1,0:T(8,128)(2,1)S(1)}, u32[]{:S(2)}, u32[]{:S(2)}) async-start(bf16[32,8,512]{2,1,0:T(8,128)(2,1)} %fusion.105), calls=%async_computation | async-start | bytes 524288 | tf_op jit(solution)/shard_map/while/body/eval_jaxpr/all_to_all | solution.py:38
  40.6 8.7 %collective-permute-start = (bf16[256,512]{1,0:T(8,128)(2,1)S(1)}, bf16[256,512]{1,0:T(8,128)(2,1)S(1)}, u32[]{:S(2)}, u32[]{:S(2)}) collective-permute-start(bf16[256,512]{1,0:T(8,128)(2,1)S(1)} %get-tuple-element.1054), channel_id=1, source_target_pairs={{0,32},{32,64},{64,96},{1,33},{33,65},{65,97},{2,34},{34,66},{66,9... | collective-permute-start | bytes 786440 | tf_op jit(solution)/shard_map/while/body/eval_jaxpr/ppermute | solution.py:10
  54.5 13.6 %all-to-all-start = ((bf16[32,8,512]{2,1,0:T(8,128)(2,1)}), bf16[32,8,512]{2,1,0:T(8,128)(2,1)S(1)}, u32[]{:S(2)}, u32[]{:S(2)}) async-start(bf16[32,8,512]{2,1,0:T(8,128)(2,1)} %fusion.105), calls=%async_computation | async-start | bytes 524288 | tf_op jit(solution)/shard_map/while/body/eval_jaxpr/all_to_all | solution.py:38
  72.4 9.7 %collective-permute-start = (bf16[256,512]{1,0:T(8,128)(2,1)S(1)}, bf16[256,512]{1,0:T(8,128)(2,1)S(1)}, u32[]{:S(2)}, u32[]{:S(2)}) collective-permute-start(bf16[256,512]{1,0:T(8,128)(2,1)S(1)} %get-tuple-element.1054), channel_id=1, source_target_pairs={{0,32},{32,64},{64,96},{1,33},{33,65},{65,97},{2,34},{34,66},{66,9... | collective-permute-start | bytes 786440 | tf_op jit(solution)/shard_map/while/body/eval_jaxpr/ppermute | solution.py:10
  87.2 13.6 %all-to-all-start = ((bf16[32,8,512]{2,1,0:T(8,128)(2,1)}), bf16[32,8,512]{2,1,0:T(8,128)(2,1)S(1)}, u32[]{:S(2)}, u32[]{:S(2)}) async-start(bf16[32,8,512]{2,1,0:T(8,128)(2,1)} %fusion.105), calls=%async_computation | async-start | bytes 524288 | tf_op jit(solution)/shard_map/while/body/eval_jaxpr/all_to_all | solution.py:38
  105.1 9.7 %collective-permute-start = (bf16[256,512]{1,0:T(8,128)(2,1)S(1)}, bf16[256,512]{1,0:T(8,128)(2,1)S(1)}, u32[]{:S(2)}, u32[]{:S(2)}) collective-permute-start(bf16[256,512]{1,0:T(8,128)(2,1)S(1)} %get-tuple-element.1054), channel_id=1, source_target_pairs={{0,32},{32,64},{64,96},{1,33},{33,65},{65,97},{2,34},{34,66},{66,9... | collective-permute-start | bytes 786440 | tf_op jit(solution)/shard_map/while/body/eval_jaxpr/ppermute | solution.py:10
  119.9 13.6 %all-to-all-start = ((bf16[32,8,512]{2,1,0:T(8,128)(2,1)}), bf16[32,8,512]{2,1,0:T(8,128)(2,1)S(1)}, u32[]{:S(2)}, u32[]{:S(2)}) async-start(bf16[32,8,512]{2,1,0:T(8,128)(2,1)} %fusion.105), calls=%async_computation | async-start | bytes 524288 | tf_op jit(solution)/shard_map/while/body/eval_jaxpr/all_to_all | solution.py:38
  137.8 9.7 %collective-permute-start = (bf16[256,512]{1,0:T(8,128)(2,1)S(1)}, bf16[256,512]{1,0:T(8,128)(2,1)S(1)}, u32[]{:S(2)}, u32[]{:S(2)}) collective-permute-start(bf16[256,512]{1,0:T(8,128)(2,1)S(1)} %get-tuple-element.1054), channel_id=1, source_target_pairs={{0,32},{32,64},{64,96},{1,33},{33,65},{65,97},{2,34},{34,66},{66,9... | collective-permute-start | bytes 786440 | tf_op jit(solution)/shard_map/while/body/eval_jaxpr/ppermute | solution.py:10
  152.6 13.6 %all-to-all-start = ((bf16[32,8,512]{2,1,0:T(8,128)(2,1)}), bf16[32,8,512]{2,1,0:T(8,128)(2,1)S(1)}, u32[]{:S(2)}, u32[]{:S(2)}) async-start(bf16[32,8,512]{2,1,0:T(8,128)(2,1)} %fusion.105), calls=%async_computation | async-start | bytes 524288 | tf_op jit(solution)/shard_map/while/body/eval_jaxpr/all_to_all | solution.py:38
  170.5 9.7 %collective-permute-start = (bf16[256,512]{1,0:T(8,128)(2,1)S(1)}, bf16[256,512]{1,0:T(8,128)(2,1)S(1)}, u32[]{:S(2)}, u32[]{:S(2)}) collective-permute-start(bf16[256,512]{1,0:T(8,128)(2,1)S(1)} %get-tuple-element.1054), channel_id=1, source_target_pairs={{0,32},{32,64},{64,96},{1,33},{33,65},{65,97},{2,34},{34,66},{66,9... | collective-permute-start | bytes 786440 | tf_op jit(solution)/shard_map/while/body/eval_jaxpr/ppermute | solution.py:10
  185.4 13.6 %all-to-all-start = ((bf16[32,8,512]{2,1,0:T(8,128)(2,1)}), bf16[32,8,512]{2,1,0:T(8,128)(2,1)S(1)}, u32[]{:S(2)}, u32[]{:S(2)}) async-start(bf16[32,8,512]{2,1,0:T(8,128)(2,1)} %fusion.105), calls=%async_computation | async-start | bytes 524288 | tf_op jit(solution)/shard_map/while/body/eval_jaxpr/all_to_all | solution.py:38
  203.2 9.7 %collective-permute-start = (bf16[256,512]{1,0:T(8,128)(2,1)S(1)}, bf16[256,512]{1,0:T(8,128)(2,1)S(1)}, u32[]{:S(2)}, u32[]{:S(2)}) collective-permute-start(bf16[256,512]{1,0:T(8,128)(2,1)S(1)} %get-tuple-element.1054), channel_id=1, source_target_pairs={{0,32},{32,64},{64,96},{1,33},{33,65},{65,97},{2,34},{34,66},{66,9... | collective-permute-start | bytes 786440 | tf_op jit(solution)/shard_map/while/body/eval_jaxpr/ppermute | solution.py:10
  218.1 13.6 %all-to-all-start = ((bf16[32,8,512]{2,1,0:T(8,128)(2,1)}), bf16[32,8,512]{2,1,0:T(8,128)(2,1)S(1)}, u32[]{:S(2)}, u32[]{:S(2)}) async-start(bf16[32,8,512]{2,1,0:T(8,128)(2,1)} %fusion.105), calls=%async_computation | async-start | bytes 524288 | tf_op jit(solution)/shard_map/while/body/eval_jaxpr/all_to_all | solution.py:38
  235.9 9.7 %collective-permute-start = (bf16[256,512]{1,0:T(8,128)(2,1)S(1)}, bf16[256,512]{1,0:T(8,128)(2,1)S(1)}, u32[]{:S(2)}, u32[]{:S(2)}) collective-permute-start(bf16[256,512]{1,0:T(8,128)(2,1)S(1)} %get-tuple-element.1054), channel_id=1, source_target_pairs={{0,32},{32,64},{64,96},{1,33},{33,65},{65,97},{2,34},{34,66},{66,9... | collective-permute-start | bytes 786440 | tf_op jit(solution)/shard_map/while/body/eval_jaxpr/ppermute | solution.py:10
  257.0 14.3 %all-to-all-start.1 = ((bf16[32,8,512]{2,1,0:T(8,128)(2,1)}), bf16[32,8,512]{2,1,0:T(8,128)(2,1)}, u32[]{:S(2)}, u32[]{:S(2)}) async-start(bf16[32,8,512]{2,1,0:T(8,128)(2,1)} %bitcast.226), calls=%async_computation.1 | async-start | bytes 524288 | tf_op jit(solution)/shard_map/while/body/eval_jaxpr/all_to_all | solution.py:95
  275.0 10.8 %collective-permute-start.1 = (bf16[256,512]{1,0:T(8,128)(2,1)S(1)}, bf16[256,512]{1,0:T(8,128)(2,1)}, u32[]{:S(2)}, u32[]{:S(2)}) collective-permute-start(bf16[256,512]{1,0:T(8,128)(2,1)S(1)} %get-tuple-element.1075), channel_id=1, source_target_pairs={{32,0},{64,32},{96,64},{33,1},{65,33},{97,65},{34,2},{66,34},{98,6... | collective-permute-start | bytes 786440 | tf_op jit(solution)/shard_map/while/body/eval_jaxpr/ppermute | solution.py:10
  293.3 14.0 %all-to-all-start.1 = ((bf16[32,8,512]{2,1,0:T(8,128)(2,1)}), bf16[32,8,512]{2,1,0:T(8,128)(2,1)}, u32[]{:S(2)}, u32[]{:S(2)}) async-start(bf16[32,8,512]{2,1,0:T(8,128)(2,1)} %bitcast.226), calls=%async_computation.1 | async-start | bytes 524288 | tf_op jit(solution)/shard_map/while/body/eval_jaxpr/all_to_all | solution.py:95
  310.9 9.7 %collective-permute-start.1 = (bf16[256,512]{1,0:T(8,128)(2,1)S(1)}, bf16[256,512]{1,0:T(8,128)(2,1)}, u32[]{:S(2)}, u32[]{:S(2)}) collective-permute-start(bf16[256,512]{1,0:T(8,128)(2,1)S(1)} %get-tuple-element.1075), channel_id=1, source_target_pairs={{32,0},{64,32},{96,64},{33,1},{65,33},{97,65},{34,2},{66,34},{98,6... | collective-permute-start | bytes 786440 | tf_op jit(solution)/shard_map/while/body/eval_jaxpr/ppermute | solution.py:10
  328.2 14.3 %all-to-all-start.1 = ((bf16[32,8,512]{2,1,0:T(8,128)(2,1)}), bf16[32,8,512]{2,1,0:T(8,128)(2,1)}, u32[]{:S(2)}, u32[]{:S(2)}) async-start(bf16[32,8,512]{2,1,0:T(8,128)(2,1)} %bitcast.226), calls=%async_computation.1 | async-start | bytes 524288 | tf_op jit(solution)/shard_map/while/body/eval_jaxpr/all_to_all | solution.py:95
  346.1 9.7 %collective-permute-start.1 = (bf16[256,512]{1,0:T(8,128)(2,1)S(1)}, bf16[256,512]{1,0:T(8,128)(2,1)}, u32[]{:S(2)}, u32[]{:S(2)}) collective-permute-start(bf16[256,512]{1,0:T(8,128)(2,1)S(1)} %get-tuple-element.1075), channel_id=1, source_target_pairs={{32,0},{64,32},{96,64},{33,1},{65,33},{97,65},{34,2},{66,34},{98,6... | collective-permute-start | bytes 786440 | tf_op jit(solution)/shard_map/while/body/eval_jaxpr/ppermute | solution.py:10
  363.4 14.3 %all-to-all-start.1 = ((bf16[32,8,512]{2,1,0:T(8,128)(2,1)}), bf16[32,8,512]{2,1,0:T(8,128)(2,1)}, u32[]{:S(2)}, u32[]{:S(2)}) async-start(bf16[32,8,512]{2,1,0:T(8,128)(2,1)} %bitcast.226), calls=%async_computation.1 | async-start | bytes 524288 | tf_op jit(solution)/shard_map/while/body/eval_jaxpr/all_to_all | solution.py:95
  381.3 9.7 %collective-permute-start.1 = (bf16[256,512]{1,0:T(8,128)(2,1)S(1)}, bf16[256,512]{1,0:T(8,128)(2,1)}, u32[]{:S(2)}, u32[]{:S(2)}) collective-permute-start(bf16[256,512]{1,0:T(8,128)(2,1)S(1)} %get-tuple-element.1075), channel_id=1, source_target_pairs={{32,0},{64,32},{96,64},{33,1},{65,33},{97,65},{34,2},{66,34},{98,6... | collective-permute-start | bytes 786440 | tf_op jit(solution)/shard_map/while/body/eval_jaxpr/ppermute | solution.py:10
  398.5 14.3 %all-to-all-start.1 = ((bf16[32,8,512]{2,1,0:T(8,128)(2,1)}), bf16[32,8,512]{2,1,0:T(8,128)(2,1)}, u32[]{:S(2)}, u32[]{:S(2)}) async-start(bf16[32,8,512]{2,1,0:T(8,128)(2,1)} %bitcast.226), calls=%async_computation.1 | async-start | bytes 524288 | tf_op jit(solution)/shard_map/while/body/eval_jaxpr/all_to_all | solution.py:95
  416.5 9.7 %collective-permute-start.1 = (bf16[256,512]{1,0:T(8,128)(2,1)S(1)}, bf16[256,512]{1,0:T(8,128)(2,1)}, u32[]{:S(2)}, u32[]{:S(2)}) collective-permute-start(bf16[256,512]{1,0:T(8,128)(2,1)S(1)} %get-tuple-element.1075), channel_id=1, source_target_pairs={{32,0},{64,32},{96,64},{33,1},{65,33},{97,65},{34,2},{66,34},{98,6... | collective-permute-start | bytes 786440 | tf_op jit(solution)/shard_map/while/body/eval_jaxpr/ppermute | solution.py:10
  433.7 14.3 %all-to-all-start.1 = ((bf16[32,8,512]{2,1,0:T(8,128)(2,1)}), bf16[32,8,512]{2,1,0:T(8,128)(2,1)}, u32[]{:S(2)}, u32[]{:S(2)}) async-start(bf16[32,8,512]{2,1,0:T(8,128)(2,1)} %bitcast.226), calls=%async_computation.1 | async-start | bytes 524288 | tf_op jit(solution)/shard_map/while/body/eval_jaxpr/all_to_all | solution.py:95
  451.7 9.7 %collective-permute-start.1 = (bf16[256,512]{1,0:T(8,128)(2,1)S(1)}, bf16[256,512]{1,0:T(8,128)(2,1)}, u32[]{:S(2)}, u32[]{:S(2)}) collective-permute-start(bf16[256,512]{1,0:T(8,128)(2,1)S(1)} %get-tuple-element.1075), channel_id=1, source_target_pairs={{32,0},{64,32},{96,64},{33,1},{65,33},{97,65},{34,2},{66,34},{98,6... | collective-permute-start | bytes 786440 | tf_op jit(solution)/shard_map/while/body/eval_jaxpr/ppermute | solution.py:10
  468.9 14.3 %all-to-all-start.1 = ((bf16[32,8,512]{2,1,0:T(8,128)(2,1)}), bf16[32,8,512]{2,1,0:T(8,128)(2,1)}, u32[]{:S(2)}, u32[]{:S(2)}) async-start(bf16[32,8,512]{2,1,0:T(8,128)(2,1)} %bitcast.226), calls=%async_computation.1 | async-start | bytes 524288 | tf_op jit(solution)/shard_map/while/body/eval_jaxpr/all_to_all | solution.py:95
  486.9 9.7 %collective-permute-start.1 = (bf16[256,512]{1,0:T(8,128)(2,1)S(1)}, bf16[256,512]{1,0:T(8,128)(2,1)}, u32[]{:S(2)}, u32[]{:S(2)}) collective-permute-start(bf16[256,512]{1,0:T(8,128)(2,1)S(1)} %get-tuple-element.1075), channel_id=1, source_target_pairs={{32,0},{64,32},{96,64},{33,1},{65,33},{97,65},{34,2},{66,34},{98,6... | collective-permute-start | bytes 786440 | tf_op jit(solution)/shard_map/while/body/eval_jaxpr/ppermute | solution.py:10
  (38 other events, 264.8 us)
Sparse Core Ops, SparseCore 0:
  499.4 103.3 all-reduce.2
where the time goes:
time: 619 us; the launch traced here: 614 us
  waiting for transfers between devices  254 us (41%)
  starting transfers between devices  110 us (18%)
  matrix products  99.4 us (16%)
  other arithmetic  80.9 us (13%)
  local copies, waits for them, and re-layouts  53 us (9%)
  between operations  14.1 us (2%)
    psum x1, waiting for transfers between devices, finish_grads(): lax.psum(grad_pair[0].astype(jnp.bfloat16), 'node').astype(jnp.float32)  103 us
    ppermute x14, waiting for transfers between devices, from_behind(): lax.ppermute(value, axis, [(source, source + steps) for source in range(f...  70.6 us
    all_to_all x7, waiting for transfers between devices, layer_forward(): lax.all_to_all(outgoing, 'node', split_axis=0, concat_axis=0, tiled=True)  47.2 us
    ppermute x14, starting transfers between devices, from_behind(): lax.ppermute(value, axis, [(source, source + steps) for source in range(f...  37.7 us
    all_to_all x7, starting transfers between devices, layer_forward(): lax.all_to_all(outgoing, 'node', split_axis=0, concat_axis=0, tiled=True)  36.7 us
    dynamic_update_slice x28, other arithmetic, put_row(): lax.dynamic_update_index_in_dim(buffer, jnp.where(valid, value, current),...  36.2 us
    all_to_all x7, starting transfers between devices, layer_backward(): lax.all_to_all(remote, 'node', split_axis=0, concat_axis=0, tiled=True)  35.8 us
    all_to_all x7, waiting for transfers between devices, layer_backward(): lax.all_to_all(remote, 'node', split_axis=0, concat_axis=0, tiled=True)  33.1 us
  transfers between devices with their start and end apart: 29, of which 29 were waited for; matrix products, arithmetic and copies ran while one was open for 12% of the time, Pallas kernels for 0%

commit v1 on v0

--- a/solution.py
+++ b/solution.py
@@ -106,7 +106,9 @@
 
 def finish_grads(grad_pair, scale):
     summed = (
-        lax.psum(grad_pair[0].astype(jnp.bfloat16), "node").astype(jnp.float32),
+        jnp.sum(lax.all_gather(grad_pair[0].astype(jnp.bfloat16), "node"), axis=0).astype(
+            jnp.float32
+        ),
         lax.psum(grad_pair[1].astype(jnp.bfloat16), "node").astype(jnp.float32),
     )
     return (summed[0] * scale, summed[1] * scale)

time: 619 us -> 698 us (1.13)
  waiting for transfers between devices: 254 us -> 326 us
  other arithmetic: 80.9 us -> 89.1 us
    all_gather x0 -> x1, waiting for transfers between devices: none -> 73.5 us  [finish_grads(): lax.all_gather(grad_pair[0].astype(jnp.bfloat16), 'node')]
    reduce_sum x0 -> x1, other arithmetic: none -> 8.8 us  [finish_grads(): jnp.sum(lax.all_gather(grad_pair[0].astype(jnp.bfloat16), 'node'), axis=0)]
    dot_general x7, matrix products: 18.1 us -> 9.35 us  [layer_backward(): lax.dot_general(hidden_in, d_pre, over_rows, preferred_element_type=jnp.f...]
    dot_general x7, matrix products: 9.37 us -> 18 us  [layer_backward(): lax.dot_general(aggregate, d_pre, over_rows, preferred_element_type=jnp.f...]
  transfers between devices with their start and end apart: 29 -> 30, of which waited for: 29 -> 30; matrix products, arithmetic and copies ran while one was open for 12% -> 11% of each run, Pallas kernels for 0% -> 0%
where the time goes in v1:
time: 698 us; the launch traced here: 693 us
  waiting for transfers between devices  326 us (47%)
  starting transfers between devices  110 us (16%)
  matrix products  99.2 us (14%)
  other arithmetic  89.1 us (13%)
  local copies, waits for them, and re-layouts  53.1 us (8%)
  between operations  14.2 us (2%)
    psum x1, waiting for transfers between devices, finish_grads(): lax.psum(grad_pair[1].astype(jnp.bfloat16), 'node').astype(jnp.float32)  101 us
    all_gather x1, waiting for transfers between devices, finish_grads(): lax.all_gather(grad_pair[0].astype(jnp.bfloat16), 'node')  73.5 us
    ppermute x14, waiting for transfers between devices, from_behind(): lax.ppermute(value, axis, [(source, source + steps) for source in range(f...  70.6 us
    all_to_all x7, waiting for transfers between devices, layer_forward(): lax.all_to_all(outgoing, 'node', split_axis=0, concat_axis=0, tiled=True)  47.2 us
    ppermute x14, starting transfers between devices, from_behind(): lax.ppermute(value, axis, [(source, source + steps) for source in range(f...  37.7 us
    all_to_all x7, starting transfers between devices, layer_forward(): lax.all_to_all(outgoing, 'node', split_axis=0, concat_axis=0, tiled=True)  36.7 us
    dynamic_update_slice x28, other arithmetic, put_row(): lax.dynamic_update_index_in_dim(buffer, jnp.where(valid, value, current),...  36.2 us
    all_to_all x7, starting transfers between devices, layer_backward(): lax.all_to_all(remote, 'node', split_axis=0, concat_axis=0, tiled=True)  35.9 us
  transfers between devices with their start and end apart: 30, of which 30 were waited for; matrix products, arithmetic and copies ran while one was open for 11% of the time, Pallas kernels for 0%

profile of v1, /device:TPU:1, one launch (start us, length us, event | category | flops | bytes accessed | tf_op | source)
XLA Modules:
  0.0 693.4 jit_solution(18045445724515416867)
XLA Ops:
  12.6 233.2 %while.44 = (s32[]{:T(128)}, bf16[256,512]{1,0:T(8,128)(2,1)S(1)}, bf16[4,256,512]{2,1,0:T(8,128)(2,1)}, bf16[4,256,512]{2,1,0:T(8,128)(2,1)}, f32[4,256,512]{2,...) while((s32[]{:T(128)}, bf16[256,512]{1,0:T(8,128)(2,1)S(1)}, ...), condition=%wide.region_1.2_spmd, body=%wide.region_0.1_spmd.sunk | while | flops 406065728 | bytes 27805224 | solution.py:168
  17.8 9.6 %all-to-all-start = ((bf16[32,8,512]{2,1,0:T(8,128)(2,1)}), bf16[32,8,512]{2,1,0:T(8,128)(2,1)S(1)}, u32[]{:S(2)}, u32[]{:S(2)}) async-start(bf16[32,8,512]{2,1,0:T(8,128)(2,1)} %fusion.105), calls=%async_computation | async-start | bytes 524288 | tf_op jit(solution)/shard_map/while/body/eval_jaxpr/all_to_all | solution.py:38
  29.7 6.6 all-to-all-done
  61.3 6.8 all-to-all-done
  94.1 6.8 all-to-all-done
  126.8 6.8 all-to-all-done
  159.6 6.8 all-to-all-done
  192.3 6.8 all-to-all-done
  225.0 6.8 all-to-all-done
  249.6 247.2 %while.45 = (s32[]{:T(128)}, bf16[256,512]{1,0:T(8,128)(2,1)}, f32[512,512]{1,0:T(8,128)}, f32[512,512]{1,0:T(8,128)}, bf16[4,256,512]{2,1,0:T(8,128)(2,1)}, /*i...) while((s32[]{:T(128)}, bf16[256,512]{1,0:T(8,128)(2,1)}, ...), condition=%wide.region_5.6_spmd.clone, body=%wide.region_3.5_spmd.clone.sunk | while | flops 700186880 | bytes 31204564 | solution.py:198
  257.2 5.2 all-to-all-start.1
  266.4 5.1 all-to-all-done.1
  277.7 8.1 %collective-permute-done.1 = bf16[256,512]{1,0:T(8,128)(2,1)} collective-permute-done((bf16[256,512]{1,0:T(8,128)(2,1)S(1)}, bf16[256,512]{1,0:T(8,128)(2,1)}, u32[]{:S(2)}, u32[]{:S(2)}) %collective-permute-start.1) | collective-permute-done | bytes 262176 | tf_op jit(solution)/shard_map/while/body/eval_jaxpr/ppermute | solution.py:10
  293.4 4.8 all-to-all-start.1
  302.7 4.7 all-to-all-done.1
  313.7 7.1 %collective-permute-done.1 = bf16[256,512]{1,0:T(8,128)(2,1)} collective-permute-done((bf16[256,512]{1,0:T(8,128)(2,1)S(1)}, bf16[256,512]{1,0:T(8,128)(2,1)}, u32[]{:S(2)}, u32[]{:S(2)}) %collective-permute-start.1) | collective-permute-done | bytes 262176 | tf_op jit(solution)/shard_map/while/body/eval_jaxpr/ppermute | solution.py:10
  328.3 5.2 all-to-all-start.1
  337.9 4.7 all-to-all-done.1
  348.9 7.1 %collective-permute-done.1 = bf16[256,512]{1,0:T(8,128)(2,1)} collective-permute-done((bf16[256,512]{1,0:T(8,128)(2,1)S(1)}, bf16[256,512]{1,0:T(8,128)(2,1)}, u32[]{:S(2)}, u32[]{:S(2)}) %collective-permute-start.1) | collective-permute-done | bytes 262176 | tf_op jit(solution)/shard_map/while/body/eval_jaxpr/ppermute | solution.py:10
  363.5 5.2 all-to-all-start.1
  384.1 7.1 %collective-permute-done.1 = bf16[256,512]{1,0:T(8,128)(2,1)} collective-permute-done((bf16[256,512]{1,0:T(8,128)(2,1)S(1)}, bf16[256,512]{1,0:T(8,128)(2,1)}, u32[]{:S(2)}, u32[]{:S(2)}) %collective-permute-start.1) | collective-permute-done | bytes 262176 | tf_op jit(solution)/shard_map/while/body/eval_jaxpr/ppermute | solution.py:10
  398.7 5.2 all-to-all-start.1
  408.3 4.7 all-to-all-done.1
  419.3 7.1 %collective-permute-done.1 = bf16[256,512]{1,0:T(8,128)(2,1)} collective-permute-done((bf16[256,512]{1,0:T(8,128)(2,1)S(1)}, bf16[256,512]{1,0:T(8,128)(2,1)}, u32[]{:S(2)}, u32[]{:S(2)}) %collective-permute-start.1) | collective-permute-done | bytes 262176 | tf_op jit(solution)/shard_map/while/body/eval_jaxpr/ppermute | solution.py:10
  433.9 5.2 all-to-all-start.1
  443.5 4.7 all-to-all-done.1
  454.5 7.1 %collective-permute-done.1 = bf16[256,512]{1,0:T(8,128)(2,1)} collective-permute-done((bf16[256,512]{1,0:T(8,128)(2,1)S(1)}, bf16[256,512]{1,0:T(8,128)(2,1)}, u32[]{:S(2)}, u32[]{:S(2)}) %collective-permute-start.1) | collective-permute-done | bytes 262176 | tf_op jit(solution)/shard_map/while/body/eval_jaxpr/ppermute | solution.py:10
  469.1 5.2 all-to-all-start.1
  489.7 7.1 %collective-permute-done.1 = bf16[256,512]{1,0:T(8,128)(2,1)} collective-permute-done((bf16[256,512]{1,0:T(8,128)(2,1)S(1)}, bf16[256,512]{1,0:T(8,128)(2,1)}, u32[]{:S(2)}, u32[]{:S(2)}) %collective-permute-start.1) | collective-permute-done | bytes 262176 | tf_op jit(solution)/shard_map/while/body/eval_jaxpr/ppermute | solution.py:10
  499.9 101.1 %all-reduce.2.cloned.1.call-done = bf16[1,512,512]{2,1,0:T(8,128)(2,1)} async-done(((bf16[1,512,512]{2,1,0:T(8,128)(2,1)}), bf16[1,512,512]{2,1,0:T(8,128)(2,1)}) %all-reduce.2.cloned.1.call-update) | async-done | bytes 524304 | tf_op jit(solution)/shard_map/psum | solution.py:112
  603.2 73.5 %all-gather.3.cloned.1.call-done = bf16[16384,512]{1,0:T(8,128)(2,1)} async-done(((bf16[512,512]{1,0:T(8,128)(2,1)}), bf16[16384,512]{1,0:T(8,128)(2,1)}) %all-gather.3.cloned.1.call-update) | async-done | bytes 16777232 | tf_op jit(solution)/shard_map/all_gather | solution.py:109
  676.6 8.8 %reduce.2 = bf16[512,512]{1,0:T(8,128)(2,1)S(1)} reduce(bf16[32,512,512]{2,1,0:T(8,128)(2,1)} %bitcast.235, bf16[]{:T(256)} %constant.228.clone.1), dimensions={0}, to_apply=%region_6.7 | reduce | flops 8126464 | bytes 17301506 | tf_op jit(solution)/shard_map/reduce_sum | solution.py:109
  (428 shorter events, 327.1 us)
Async XLA Ops:
  7.2 238.6 %copy-start = (bf16[512,172]{0,1:T(8,128)(2,1)S(1)}, bf16[512,172]{0,1:T(8,128)(2,1)}, u32[]{:S(2)}) copy-start(bf16[512,172]{0,1:T(8,128)(2,1)} %param.17) | copy-start | bytes 528388
  7.2 593.8 %all-reduce.2.cloned.1.call-start = ((), (), s32[]{:S(2)}) async-start(), calls=%async_computation.2 | async-start | bytes 1048576 | tf_op jit(solution)/shard_map/psum | solution.py:112
  12.6 233.7 %copy-start.10 = (s32[4,256]{1,0:T(4,128)S(1)}, s32[4,256]{1,0:T(4,128)}, u32[]{:S(2)}) copy-start(s32[4,256]{1,0:T(4,128)} %param.18) | copy-start | bytes 12292
  17.8 18.6 %all-to-all-start = ((bf16[32,8,512]{2,1,0:T(8,128)(2,1)}), bf16[32,8,512]{2,1,0:T(8,128)(2,1)S(1)}, u32[]{:S(2)}, u32[]{:S(2)}) async-start(bf16[32,8,512]{2,1,0:T(8,128)(2,1)} %fusion.105), calls=%async_computation | async-start | bytes 524288 | tf_op jit(solution)/shard_map/while/body/eval_jaxpr/all_to_all | solution.py:38
  40.6 8.7 %collective-permute-start = (bf16[256,512]{1,0:T(8,128)(2,1)S(1)}, bf16[256,512]{1,0:T(8,128)(2,1)S(1)}, u32[]{:S(2)}, u32[]{:S(2)}) collective-permute-start(bf16[256,512]{1,0:T(8,128)(2,1)S(1)} %get-tuple-element.1050), channel_id=1, source_target_pairs={{0,32},{32,64},{64,96},{1,33},{33,65},{65,97},{2,34},{34,66},{66,9... | collective-permute-start | bytes 786440 | tf_op jit(solution)/shard_map/while/body/eval_jaxpr/ppermute | solution.py:10
  54.5 13.6 %all-to-all-start = ((bf16[32,8,512]{2,1,0:T(8,128)(2,1)}), bf16[32,8,512]{2,1,0:T(8,128)(2,1)S(1)}, u32[]{:S(2)}, u32[]{:S(2)}) async-start(bf16[32,8,512]{2,1,0:T(8,128)(2,1)} %fusion.105), calls=%async_computation | async-start | bytes 524288 | tf_op jit(solution)/shard_map/while/body/eval_jaxpr/all_to_all | solution.py:38
  72.3 9.7 %collective-permute-start = (bf16[256,512]{1,0:T(8,128)(2,1)S(1)}, bf16[256,512]{1,0:T(8,128)(2,1)S(1)}, u32[]{:S(2)}, u32[]{:S(2)}) collective-permute-start(bf16[256,512]{1,0:T(8,128)(2,1)S(1)} %get-tuple-element.1050), channel_id=1, source_target_pairs={{0,32},{32,64},{64,96},{1,33},{33,65},{65,97},{2,34},{34,66},{66,9... | collective-permute-start | bytes 786440 | tf_op jit(solution)/shard_map/while/body/eval_jaxpr/ppermute | solution.py:10
  87.2 13.6 %all-to-all-start = ((bf16[32,8,512]{2,1,0:T(8,128)(2,1)}), bf16[32,8,512]{2,1,0:T(8,128)(2,1)S(1)}, u32[]{:S(2)}, u32[]{:S(2)}) async-start(bf16[32,8,512]{2,1,0:T(8,128)(2,1)} %fusion.105), calls=%async_computation | async-start | bytes 524288 | tf_op jit(solution)/shard_map/while/body/eval_jaxpr/all_to_all | solution.py:38
  105.1 9.7 %collective-permute-start = (bf16[256,512]{1,0:T(8,128)(2,1)S(1)}, bf16[256,512]{1,0:T(8,128)(2,1)S(1)}, u32[]{:S(2)}, u32[]{:S(2)}) collective-permute-start(bf16[256,512]{1,0:T(8,128)(2,1)S(1)} %get-tuple-element.1050), channel_id=1, source_target_pairs={{0,32},{32,64},{64,96},{1,33},{33,65},{65,97},{2,34},{34,66},{66,9... | collective-permute-start | bytes 786440 | tf_op jit(solution)/shard_map/while/body/eval_jaxpr/ppermute | solution.py:10
  119.9 13.6 %all-to-all-start = ((bf16[32,8,512]{2,1,0:T(8,128)(2,1)}), bf16[32,8,512]{2,1,0:T(8,128)(2,1)S(1)}, u32[]{:S(2)}, u32[]{:S(2)}) async-start(bf16[32,8,512]{2,1,0:T(8,128)(2,1)} %fusion.105), calls=%async_computation | async-start | bytes 524288 | tf_op jit(solution)/shard_map/while/body/eval_jaxpr/all_to_all | solution.py:38
  137.8 9.7 %collective-permute-start = (bf16[256,512]{1,0:T(8,128)(2,1)S(1)}, bf16[256,512]{1,0:T(8,128)(2,1)S(1)}, u32[]{:S(2)}, u32[]{:S(2)}) collective-permute-start(bf16[256,512]{1,0:T(8,128)(2,1)S(1)} %get-tuple-element.1050), channel_id=1, source_target_pairs={{0,32},{32,64},{64,96},{1,33},{33,65},{65,97},{2,34},{34,66},{66,9... | collective-permute-start | bytes 786440 | tf_op jit(solution)/shard_map/while/body/eval_jaxpr/ppermute | solution.py:10
  152.7 13.6 %all-to-all-start = ((bf16[32,8,512]{2,1,0:T(8,128)(2,1)}), bf16[32,8,512]{2,1,0:T(8,128)(2,1)S(1)}, u32[]{:S(2)}, u32[]{:S(2)}) async-start(bf16[32,8,512]{2,1,0:T(8,128)(2,1)} %fusion.105), calls=%async_computation | async-start | bytes 524288 | tf_op jit(solution)/shard_map/while/body/eval_jaxpr/all_to_all | solution.py:38
  170.6 9.7 %collective-permute-start = (bf16[256,512]{1,0:T(8,128)(2,1)S(1)}, bf16[256,512]{1,0:T(8,128)(2,1)S(1)}, u32[]{:S(2)}, u32[]{:S(2)}) collective-permute-start(bf16[256,512]{1,0:T(8,128)(2,1)S(1)} %get-tuple-element.1050), channel_id=1, source_target_pairs={{0,32},{32,64},{64,96},{1,33},{33,65},{65,97},{2,34},{34,66},{66,9... | collective-permute-start | bytes 786440 | tf_op jit(solution)/shard_map/while/body/eval_jaxpr/ppermute | solution.py:10
  185.4 13.6 %all-to-all-start = ((bf16[32,8,512]{2,1,0:T(8,128)(2,1)}), bf16[32,8,512]{2,1,0:T(8,128)(2,1)S(1)}, u32[]{:S(2)}, u32[]{:S(2)}) async-start(bf16[32,8,512]{2,1,0:T(8,128)(2,1)} %fusion.105), calls=%async_computation | async-start | bytes 524288 | tf_op jit(solution)/shard_map/while/body/eval_jaxpr/all_to_all | solution.py:38
  203.3 9.7 %collective-permute-start = (bf16[256,512]{1,0:T(8,128)(2,1)S(1)}, bf16[256,512]{1,0:T(8,128)(2,1)S(1)}, u32[]{:S(2)}, u32[]{:S(2)}) collective-permute-start(bf16[256,512]{1,0:T(8,128)(2,1)S(1)} %get-tuple-element.1050), channel_id=1, source_target_pairs={{0,32},{32,64},{64,96},{1,33},{33,65},{65,97},{2,34},{34,66},{66,9... | collective-permute-start | bytes 786440 | tf_op jit(solution)/shard_map/while/body/eval_jaxpr/ppermute | solution.py:10
  218.2 13.6 %all-to-all-start = ((bf16[32,8,512]{2,1,0:T(8,128)(2,1)}), bf16[32,8,512]{2,1,0:T(8,128)(2,1)S(1)}, u32[]{:S(2)}, u32[]{:S(2)}) async-start(bf16[32,8,512]{2,1,0:T(8,128)(2,1)} %fusion.105), calls=%async_computation | async-start | bytes 524288 | tf_op jit(solution)/shard_map/while/body/eval_jaxpr/all_to_all | solution.py:38
  236.0 9.7 %collective-permute-start = (bf16[256,512]{1,0:T(8,128)(2,1)S(1)}, bf16[256,512]{1,0:T(8,128)(2,1)S(1)}, u32[]{:S(2)}, u32[]{:S(2)}) collective-permute-start(bf16[256,512]{1,0:T(8,128)(2,1)S(1)} %get-tuple-element.1050), channel_id=1, source_target_pairs={{0,32},{32,64},{64,96},{1,33},{33,65},{65,97},{2,34},{34,66},{66,9... | collective-permute-start | bytes 786440 | tf_op jit(solution)/shard_map/while/body/eval_jaxpr/ppermute | solution.py:10
  257.2 14.3 %all-to-all-start.1 = ((bf16[32,8,512]{2,1,0:T(8,128)(2,1)}), bf16[32,8,512]{2,1,0:T(8,128)(2,1)}, u32[]{:S(2)}, u32[]{:S(2)}) async-start(bf16[32,8,512]{2,1,0:T(8,128)(2,1)} %bitcast.227), calls=%async_computation.1 | async-start | bytes 524288 | tf_op jit(solution)/shard_map/while/body/eval_jaxpr/all_to_all | solution.py:95
  275.1 10.8 %collective-permute-start.1 = (bf16[256,512]{1,0:T(8,128)(2,1)S(1)}, bf16[256,512]{1,0:T(8,128)(2,1)}, u32[]{:S(2)}, u32[]{:S(2)}) collective-permute-start(bf16[256,512]{1,0:T(8,128)(2,1)S(1)} %get-tuple-element.1071), channel_id=1, source_target_pairs={{32,0},{64,32},{96,64},{33,1},{65,33},{97,65},{34,2},{66,34},{98,6... | collective-permute-start | bytes 786440 | tf_op jit(solution)/shard_map/while/body/eval_jaxpr/ppermute | solution.py:10
  293.4 14.0 %all-to-all-start.1 = ((bf16[32,8,512]{2,1,0:T(8,128)(2,1)}), bf16[32,8,512]{2,1,0:T(8,128)(2,1)}, u32[]{:S(2)}, u32[]{:S(2)}) async-start(bf16[32,8,512]{2,1,0:T(8,128)(2,1)} %bitcast.227), calls=%async_computation.1 | async-start | bytes 524288 | tf_op jit(solution)/shard_map/while/body/eval_jaxpr/all_to_all | solution.py:95
  311.0 9.7 %collective-permute-start.1 = (bf16[256,512]{1,0:T(8,128)(2,1)S(1)}, bf16[256,512]{1,0:T(8,128)(2,1)}, u32[]{:S(2)}, u32[]{:S(2)}) collective-permute-start(bf16[256,512]{1,0:T(8,128)(2,1)S(1)} %get-tuple-element.1071), channel_id=1, source_target_pairs={{32,0},{64,32},{96,64},{33,1},{65,33},{97,65},{34,2},{66,34},{98,6... | collective-permute-start | bytes 786440 | tf_op jit(solution)/shard_map/while/body/eval_jaxpr/ppermute | solution.py:10
  328.3 14.3 %all-to-all-start.1 = ((bf16[32,8,512]{2,1,0:T(8,128)(2,1)}), bf16[32,8,512]{2,1,0:T(8,128)(2,1)}, u32[]{:S(2)}, u32[]{:S(2)}) async-start(bf16[32,8,512]{2,1,0:T(8,128)(2,1)} %bitcast.227), calls=%async_computation.1 | async-start | bytes 524288 | tf_op jit(solution)/shard_map/while/body/eval_jaxpr/all_to_all | solution.py:95
  346.2 9.7 %collective-permute-start.1 = (bf16[256,512]{1,0:T(8,128)(2,1)S(1)}, bf16[256,512]{1,0:T(8,128)(2,1)}, u32[]{:S(2)}, u32[]{:S(2)}) collective-permute-start(bf16[256,512]{1,0:T(8,128)(2,1)S(1)} %get-tuple-element.1071), channel_id=1, source_target_pairs={{32,0},{64,32},{96,64},{33,1},{65,33},{97,65},{34,2},{66,34},{98,6... | collective-permute-start | bytes 786440 | tf_op jit(solution)/shard_map/while/body/eval_jaxpr/ppermute | solution.py:10
  363.5 14.3 %all-to-all-start.1 = ((bf16[32,8,512]{2,1,0:T(8,128)(2,1)}), bf16[32,8,512]{2,1,0:T(8,128)(2,1)}, u32[]{:S(2)}, u32[]{:S(2)}) async-start(bf16[32,8,512]{2,1,0:T(8,128)(2,1)} %bitcast.227), calls=%async_computation.1 | async-start | bytes 524288 | tf_op jit(solution)/shard_map/while/body/eval_jaxpr/all_to_all | solution.py:95
  381.4 9.7 %collective-permute-start.1 = (bf16[256,512]{1,0:T(8,128)(2,1)S(1)}, bf16[256,512]{1,0:T(8,128)(2,1)}, u32[]{:S(2)}, u32[]{:S(2)}) collective-permute-start(bf16[256,512]{1,0:T(8,128)(2,1)S(1)} %get-tuple-element.1071), channel_id=1, source_target_pairs={{32,0},{64,32},{96,64},{33,1},{65,33},{97,65},{34,2},{66,34},{98,6... | collective-permute-start | bytes 786440 | tf_op jit(solution)/shard_map/while/body/eval_jaxpr/ppermute | solution.py:10
  398.7 14.3 %all-to-all-start.1 = ((bf16[32,8,512]{2,1,0:T(8,128)(2,1)}), bf16[32,8,512]{2,1,0:T(8,128)(2,1)}, u32[]{:S(2)}, u32[]{:S(2)}) async-start(bf16[32,8,512]{2,1,0:T(8,128)(2,1)} %bitcast.227), calls=%async_computation.1 | async-start | bytes 524288 | tf_op jit(solution)/shard_map/while/body/eval_jaxpr/all_to_all | solution.py:95
  416.6 9.7 %collective-permute-start.1 = (bf16[256,512]{1,0:T(8,128)(2,1)S(1)}, bf16[256,512]{1,0:T(8,128)(2,1)}, u32[]{:S(2)}, u32[]{:S(2)}) collective-permute-start(bf16[256,512]{1,0:T(8,128)(2,1)S(1)} %get-tuple-element.1071), channel_id=1, source_target_pairs={{32,0},{64,32},{96,64},{33,1},{65,33},{97,65},{34,2},{66,34},{98,6... | collective-permute-start | bytes 786440 | tf_op jit(solution)/shard_map/while/body/eval_jaxpr/ppermute | solution.py:10
  433.9 14.3 %all-to-all-start.1 = ((bf16[32,8,512]{2,1,0:T(8,128)(2,1)}), bf16[32,8,512]{2,1,0:T(8,128)(2,1)}, u32[]{:S(2)}, u32[]{:S(2)}) async-start(bf16[32,8,512]{2,1,0:T(8,128)(2,1)} %bitcast.227), calls=%async_computation.1 | async-start | bytes 524288 | tf_op jit(solution)/shard_map/while/body/eval_jaxpr/all_to_all | solution.py:95
  451.8 9.7 %collective-permute-start.1 = (bf16[256,512]{1,0:T(8,128)(2,1)S(1)}, bf16[256,512]{1,0:T(8,128)(2,1)}, u32[]{:S(2)}, u32[]{:S(2)}) collective-permute-start(bf16[256,512]{1,0:T(8,128)(2,1)S(1)} %get-tuple-element.1071), channel_id=1, source_target_pairs={{32,0},{64,32},{96,64},{33,1},{65,33},{97,65},{34,2},{66,34},{98,6... | collective-permute-start | bytes 786440 | tf_op jit(solution)/shard_map/while/body/eval_jaxpr/ppermute | solution.py:10
  469.1 14.3 %all-to-all-start.1 = ((bf16[32,8,512]{2,1,0:T(8,128)(2,1)}), bf16[32,8,512]{2,1,0:T(8,128)(2,1)}, u32[]{:S(2)}, u32[]{:S(2)}) async-start(bf16[32,8,512]{2,1,0:T(8,128)(2,1)} %bitcast.227), calls=%async_computation.1 | async-start | bytes 524288 | tf_op jit(solution)/shard_map/while/body/eval_jaxpr/all_to_all | solution.py:95
  487.1 9.7 %collective-permute-start.1 = (bf16[256,512]{1,0:T(8,128)(2,1)S(1)}, bf16[256,512]{1,0:T(8,128)(2,1)}, u32[]{:S(2)}, u32[]{:S(2)}) collective-permute-start(bf16[256,512]{1,0:T(8,128)(2,1)S(1)} %get-tuple-element.1071), channel_id=1, source_target_pairs={{32,0},{64,32},{96,64},{33,1},{65,33},{97,65},{34,2},{66,34},{98,6... | collective-permute-start | bytes 786440 | tf_op jit(solution)/shard_map/while/body/eval_jaxpr/ppermute | solution.py:10
  499.0 177.7 %all-gather.3.cloned.1.call-start = ((), (), s32[]{:S(2)}) async-start(), calls=%async_computation.3 | async-start | bytes 17301504 | tf_op jit(solution)/shard_map/all_gather | solution.py:109
  (40 other events, 286.7 us)
Sparse Core Ops, SparseCore 0:
  499.1 101.8 all-reduce.1
  604.1 72.4 all-gather.2
